TPU v7x, 32 devices: a whole 2x2x4 slice. The times are simulated.
32 devices in a mesh: groups: 2 (over y), wide: 4 (over z), narrow: 4 (over x, core).
Axes of the slice: x: 2, y: 2, z: 4, core: 2. Of those that a mesh axis runs over, the one named last changes fastest.
Arguments:
- tokens: bfloat16 [512, 4096], P(('groups', 'wide'), 'narrow'), parts along dimension 0, may hold values from -6 to 6
- routes: int32 [512, 8], P(('groups', 'wide')), parts along dimension 0, may hold values from 0 to 15, all different within a row; in each aligned block of 64 rows (0 to 63, 64 to 127, ...) at most 40 rows name the same one
- gate_weights: float32 [512, 8], P(('groups', 'wide')), parts along dimension 0, may hold values from 0.05 to 1
- delta_of: int32 [16], replicated, may hold values from 0 to 15, each once
- base_gate: bfloat16 [4096, 1536], P('wide', 'narrow'), may hold values from -0.09375 to 0.09375
- base_up: bfloat16 [4096, 1536], P('wide', 'narrow'), may hold values from -0.09375 to 0.09375
- base_down: bfloat16 [1536, 4096], P('wide', 'narrow'), may hold values from -0.15625 to 0.15625
- gate_left: bfloat16 [16, 4096, 32], P('wide', 'narrow'), may hold values from -0.09375 to 0.09375
- gate_right: bfloat16 [16, 32, 1536], P('wide', None, 'narrow'), may hold values from -0.5 to 0.5
- up_left: bfloat16 [16, 4096, 32], P('wide', 'narrow'), may hold values from -0.09375 to 0.09375
- up_right: bfloat16 [16, 32, 1536], P('wide', None, 'narrow'), may hold values from -0.5 to 0.5
- down_left: bfloat16 [16, 1536, 32], P('wide', 'narrow'), may hold values from -0.15625 to 0.15625
- down_right: bfloat16 [16, 32, 4096], P('wide', None, 'narrow'), may hold values from -0.5 to 0.5
Outputs:
- mixed_out: bfloat16 [512, 4096], P(('groups', 'wide'), 'narrow'), parts along dimension 0
There are 2 independent parts, one for each index of `groups`. A program takes and returns all parts, laid end to end along the dimension named above; an argument that names none is the same for every part. Nothing has to cross between parts.
Inputs may be any that keep to these rules, and one draw needn't show every extreme that they name: `routes`: in each aligned block of 64 rows (the rows of one index of wide) no expert is named by more than 40 rows, and in some block some expert is named by exactly 40 rows.
All inputs are finite; a program needn't handle non-finite values.
Results may differ from a plain program's by a relative error of at most 0.0053.
Values may be sent and summed in bfloat16 or wider, within the bound.
A program may use at most 64 MiB of HBM per device.

v0:
```python
import jax
import jax.numpy as jnp
from jax import lax
from jax.experimental import pallas as pl
from jax.experimental.pallas import tpu as pltpu
from jax.sharding import PartitionSpec as P


def dot32(a, b):
    return jnp.dot(a, b, preferred_element_type=jnp.float32)


def dot32t(a, b):
    return lax.dot_general(a, b, (((1,), (1,)), ((), ())), preferred_element_type=jnp.float32)


PLANE = 4

LANES = 128


def kernel(
    tok, routes, shares, delta, bg_hbm, bu_hbm, bd_hbm, gl_hbm, gr, ul_hbm, ur, dl, dr_hbm, out,
    wt, bgu, lefts, bd, dr,
    xcol, xw, wts, gsend, grecv, gown, gred, gall, apart, asend, arecv, afin,
    hacc, hsend, hrecv, hpl, bpart, bsend, brecv, bfin, osend, orecv, oown,
    tok_s, tok_r, wt_s, wt_r, bs_s, bs_r, g_s, g_r, ga_s, ga_r, a_s, a_r,
    h_s, h_r, hb_s, hb_r, b_s, b_r, o_s, o_r, in_s,
):
    bf16, f32 = jnp.bfloat16, jnp.float32
    count = PLANE
    w, n = lax.axis_index("wide"), lax.axis_index("narrow")
    exp_here, rank, cols = gr.shape
    span = exp_here * rank
    loads = [
        pltpu.make_async_copy(gl_hbm, lefts.at[pl.ds(0, span)], in_s.at[0]),
        pltpu.make_async_copy(ul_hbm, lefts.at[pl.ds(span, span)], in_s.at[1]),
    ]
    chunk = LANES if cols % LANES == 0 else cols
    chunks = cols // chunk
    for c in range(chunks):
        for k, base in enumerate((bg_hbm, bu_hbm)):
            place = bgu.at[:, pl.ds((2 * c + k) * chunk, chunk)]
            loads.append(pltpu.make_async_copy(base.at[:, pl.ds(c * chunk, chunk)], place, in_s.at[2 + 2 * c + k]))
    loads.append(pltpu.make_async_copy(bd_hbm, bd, in_s.at[2 + 2 * chunks]))
    loads.append(pltpu.make_async_copy(dr_hbm, dr, in_s.at[3 + 2 * chunks]))
    for load in loads:
        load.start()
    pair = n + 1 - 2 * lax.rem(n, 2)
    across = lax.rem(n + 2, count)
    root = n == w
    relay = n == lax.rem(w + 2, count)

    def up_of(d):
        return lax.rem(w + d, count)

    def copy(src, dst, ss, rs, axis, peer):
        return pltpu.make_async_remote_copy(
            src_ref=src, dst_ref=dst, send_sem=ss, recv_sem=rs,
            device_id={axis: peer}, device_id_type=pl.DeviceIdType.MESH,
        )

    barrier = pltpu.get_barrier_semaphore()
    for d in range(1, count):
        pl.semaphore_signal(barrier, inc=1, device_id={"wide": up_of(d)}, device_id_type=pl.DeviceIdType.MESH)
    for peer in (pair, across):
        pl.semaphore_signal(barrier, inc=1, device_id={"narrow": peer}, device_id_type=pl.DeviceIdType.MESH)
    pl.semaphore_wait(barrier, count + 1)

    def tok_copy(d):
        return copy(tok, xcol.at[w], tok_s.at[d], tok_r.at[d], "wide", up_of(d))

    def wt_copy(d):
        return copy(wt, wts.at[w], wt_s.at[d], wt_r.at[d], "wide", up_of(d))

    def pair_copy(d, src):
        return copy(src, xw.at[up_of(count - d)], bs_s.at[d, 0], bs_r.at[d], "narrow", pair)

    def across_copy(d, src):
        return copy(src, xw.at[up_of(count - d)], bs_s.at[d, 1], bs_r.at[d], "narrow", across)

    for d in range(1, count):
        tok_copy(d).start()

    def g_copy(d, c, peer, slot):
        part = pl.ds(2 * c * chunk, 2 * chunk)
        return copy(gsend.at[peer, :, part], grecv.at[slot, :, part], g_s.at[d, c], g_r.at[d, c], "wide", peer)

    named, ids = routes[...], jnp.zeros(routes.shape, jnp.int32)
    for e in range(delta.shape[0]):
        ids = jnp.where(named == e, delta[e], ids)
    sets = lax.broadcasted_iota(jnp.int32, (wt.shape[1], wt.shape[0]), 0)
    table = jnp.zeros(sets.shape, f32)
    for k in range(routes.shape[0]):
        table = table + jnp.where(sets == ids[k : k + 1], shares[k : k + 1, :], 0.0)
    wt[...] = table.T
    for load in loads[:-2]:
        load.wait()

    def low(rows, b):
        apart[b] = dot32t(rows, lefts[...])

    for d in range(count):
        b = up_of(count - d)
        if d > 0:
            tok_copy(d).wait_recv()
        mine = tok if d == 0 else xcol.at[b]

        @pl.when(root)
        def _():
            across_copy(d, mine).start()
            pair_copy(d, mine).start()
            xw[b] = mine[...]

        low(mine[...], b)

        @pl.when(jnp.logical_not(root))
        def _():
            pair_copy(d, xw.at[b]).wait_recv()

        @pl.when(relay)
        def _():
            pair_copy(d, xw.at[b]).start()

        rows = xw[b]
        both = dot32(rows, bgu[...])
        if d == 0:
            gown[...] = both
            for k in range(1, count):
                wt_copy(k).start()
        else:
            gsend[b] = both.astype(bf16)
            for c in range(chunks):
                g_copy(d, c, b, w).start()

    def a_copy(k):
        return copy(asend.at[k], arecv.at[k], a_s.at[k], a_r.at[k], "narrow", (pair, across)[k])

    asend[0] = apart[...].astype(bf16)
    a_copy(0).start()
    a_copy(0).wait_recv()
    apart[...] = apart[...] + arecv[0].astype(f32)
    asend[1] = apart[...].astype(bf16)
    a_copy(1).start()

    def ga_copy(d, c):
        part = pl.ds(2 * c * chunk, 2 * chunk)
        return copy(gred.at[:, part], gall.at[w, :, part], ga_s.at[d, c], ga_r.at[d, c], "wide", up_of(d))

    for c in range(chunks):
        part = slice(2 * c * chunk, 2 * (c + 1) * chunk)
        total = gown[:, part]
        for d in range(1, count):
            g_copy(d, c, up_of(d), up_of(d)).wait_recv()
            total = total + grecv[up_of(d), :, part].astype(f32)
        gown[:, part] = total
        gred[:, part] = total.astype(bf16)
        for d in range(1, count):
            ga_copy(d, c).start()

    a_copy(1).wait_recv()
    afin[...] = (apart[...] + arecv[1].astype(f32)).astype(bf16)

    def h_copy(slot, c, target):
        part = pl.ds(c * chunk, chunk)
        return copy(hsend.at[:, :, part], hrecv.at[slot, :, :, part], h_s.at[c], h_r.at[slot, c], "wide", target)

    for c in range(chunks):
        gate_part = slice(2 * c * chunk, (2 * c + 1) * chunk)
        up_part = slice((2 * c + 1) * chunk, 2 * (c + 1) * chunk)
        part = slice(c * chunk, (c + 1) * chunk)
        for d in range(count):
            b = up_of(count - d)
            if d > 0:
                ga_copy(d, c).wait_recv()
                if c == 0:
                    wt_copy(d).wait_recv()
                gates, ups = gall[b, :, gate_part].astype(f32), gall[b, :, up_part].astype(f32)
                scales = wts[b]
            else:
                gates, ups = gown[:, gate_part], gown[:, up_part]
                scales = wt[...]
            ids = lax.broadcasted_iota(jnp.int32, scales.shape, 1)
            thin_rows = afin[b]
            acc = None
            for e in range(exp_here):
                scale = jnp.sum(jnp.where(ids == w * exp_here + e, scales, 0.0), axis=1, keepdims=True)
                own = slice(e * rank, (e + 1) * rank)
                gate = gates + dot32(thin_rows[:, own], gr[e, :, part])
                up = ups + dot32(thin_rows[:, span + e * rank : span + (e + 1) * rank], ur[e, :, part])
                hidden = gate / (1.0 + jnp.exp(-gate)) * up * scale
                acc = hidden if acc is None else acc + hidden
                thin = dot32t(hidden.astype(bf16), dl[e, :, part])
                bpart[b, :, own] = thin if c == 0 else bpart[b, :, own] + thin
            hacc[b, :, part] = acc
            hsend[b, :, part] = acc.astype(bf16)

        @pl.when(jnp.logical_not(root))
        def _():
            h_copy(w, c, n).start()

    def b_copy(k):
        return copy(bsend.at[k], brecv.at[k], b_s.at[k], b_r.at[k], "narrow", (pair, across)[k])

    bsend[0] = bpart[...].astype(bf16)
    b_copy(0).start()
    b_copy(0).wait_recv()
    bpart[...] = bpart[...] + brecv[0].astype(f32)
    bsend[1] = bpart[...].astype(bf16)
    b_copy(1).start()
    b_copy(1).wait_recv()
    bfin[...] = (bpart[...] + brecv[1].astype(f32)).astype(bf16)

    def hpair(d):
        b = up_of(count - d)
        return copy(hpl.at[b], hpl.at[b], hb_s.at[0, d], hb_r.at[d], "narrow", pair)

    def hacross(d):
        b = up_of(count - d)
        return copy(hpl.at[b], hpl.at[b], hb_s.at[1, d], hb_r.at[d], "narrow", across)

    for load in loads[-2:]:
        load.wait()

    for d in (2, 1, 3, 0):
        b = up_of(count - d)

        @pl.when(root)
        def _():
            whole = hacc[b]
            for k in range(1, count):
                src = up_of(k)
                if d == 2:
                    for c in range(chunks):
                        h_copy(src, c, src).wait_recv()
                whole = whole + hrecv[src, b].astype(f32)
            hpl[b] = whole.astype(bf16)
            hacross(d).start()
            hpair(d).start()

        @pl.when(jnp.logical_not(root))
        def _():
            hpair(d).wait_recv()

        @pl.when(relay)
        def _():
            hpair(d).start()

        part = dot32(hpl[b], bd[...]) + dot32(bfin[b], dr[...])
        if d == 0:
            oown[...] = part
        else:
            osend[b] = part.astype(bf16)
            copy(osend.at[b], orecv.at[w], o_s.at[d], o_r.at[d], "wide", b).start()
    total = oown[...]
    for d in (1, 3, 2):
        s = up_of(d)
        copy(osend.at[s], orecv.at[s], o_s.at[d], o_r.at[d], "wide", s).wait_recv()
        total = total + orecv[s].astype(f32)
    out[...] = total.astype(bf16)

    for d in range(1, count):
        b = up_of(count - d)
        tok_copy(d).wait_send()
        wt_copy(d).wait_send()
        for c in range(chunks):
            ga_copy(d, c).wait_send()
            g_copy(d, c, b, w).wait_send()
        copy(osend.at[b], orecv.at[w], o_s.at[d], o_r.at[d], "wide", b).wait_send()
    for k in range(2):
        a_copy(k).wait_send()
        b_copy(k).wait_send()

    @pl.when(root)
    def _():
        for d in range(count):
            src = tok if d == 0 else xcol.at[up_of(count - d)]
            across_copy(d, src).wait_send()
            pair_copy(d, src).wait_send()
            hacross(d).wait_send()
            hpair(d).wait_send()

    @pl.when(relay)
    def _():
        for d in range(count):
            pair_copy(d, xw.at[up_of(count - d)]).wait_send()
            hpair(d).wait_send()

    @pl.when(jnp.logical_not(root))
    def _():
        for c in range(chunks):
            h_copy(w, c, n).wait_send()


def fused(tokens, routes, shares, delta, bg, bu, bd, gl, gr, ul, ur, dl, dr):
    bf16, f32 = jnp.bfloat16, jnp.float32
    count = PLANE
    rows, feats = tokens.shape
    depth, cols = bg.shape
    exp_here, rank, _ = gr.shape
    span = exp_here * rank
    lanes = -(-delta.shape[0] // LANES) * LANES
    chunks = cols // LANES if cols % LANES == 0 else 1
    sem = pltpu.SemaphoreType.DMA
    vm = pltpu.VMEM
    out_feats = bd.shape[1]
    vmem, hbm = pl.BlockSpec(memory_space=pltpu.VMEM), pl.BlockSpec(memory_space=pl.ANY)
    return pl.pallas_call(
        kernel,
        out_shape=jax.ShapeDtypeStruct((rows, out_feats), bf16),
        in_specs=[
            vmem, vmem, vmem, pl.BlockSpec(memory_space=pltpu.SMEM),
            hbm, hbm, hbm, hbm, vmem, hbm, vmem, vmem, hbm,
        ],
        out_specs=pl.BlockSpec(memory_space=pltpu.VMEM),
        scratch_shapes=[
            vm((rows, lanes), f32),
            vm((depth, 2 * cols), bf16),
            vm((2 * span, feats), bf16),
            vm(bd.shape, bf16),
            vm((span, out_feats), bf16),
            vm((count, rows, feats), bf16),
            vm((count, rows, feats), bf16),
            vm((count, rows, lanes), f32),
            vm((count, rows, 2 * cols), bf16),
            vm((count, rows, 2 * cols), bf16),
            vm((rows, 2 * cols), f32),
            vm((rows, 2 * cols), bf16),
            vm((count, rows, 2 * cols), bf16),
            vm((count, rows, 2 * span), f32),
            vm((2, count, rows, 2 * span), bf16),
            vm((2, count, rows, 2 * span), bf16),
            vm((count, rows, 2 * span), bf16),
            vm((count, rows, cols), f32),
            vm((count, rows, cols), bf16),
            vm((count, count, rows, cols), bf16),
            vm((count, rows, cols), bf16),
            vm((count, rows, span), f32),
            vm((2, count, rows, span), bf16),
            vm((2, count, rows, span), bf16),
            vm((count, rows, span), bf16),
            vm((count, rows, out_feats), bf16),
            vm((count, rows, out_feats), bf16),
            vm((rows, out_feats), f32),
            sem((count,)), sem((count,)), sem((count,)), sem((count,)),
            sem((count, 2)), sem((count,)),
            sem((count, chunks)), sem((count, chunks)), sem((count, chunks)), sem((count, chunks)),
            sem((2,)), sem((2,)),
            sem((chunks,)), sem((count, chunks)), sem((2, count)), sem((count,)),
            sem((2,)), sem((2,)), sem((count,)), sem((count,)), sem((4 + 2 * chunks,)),
        ],
        compiler_params=pltpu.CompilerParams(collective_id=0, has_side_effects=True, vmem_limit_bytes=60 * 1024 * 1024),
    )(
        tokens, routes.T, shares.T, delta, bg, bu, bd,
        jnp.swapaxes(gl, 1, 2).reshape(span, feats), gr,
        jnp.swapaxes(ul, 1, 2).reshape(span, feats), ur,
        jnp.swapaxes(dl, 1, 2), dr.reshape(span, out_feats),
    )


def shards(
    tokens,
    routes,
    gate_weights,
    delta_of,
    base_gate,
    base_up,
    base_down,
    gate_left,
    gate_right,
    up_left,
    up_right,
    down_left,
    down_right,
):
    if lax.axis_size("narrow") == PLANE and lax.axis_size("wide") == PLANE:
        return fused(
            tokens, routes, gate_weights, delta_of, base_gate, base_up, base_down,
            gate_left, gate_right, up_left, up_right, down_left, down_right,
        )
    exp_here, _, rank = gate_left.shape
    experts = delta_of.shape[0]
    mine = lax.axis_index("wide")
    bf16 = jnp.bfloat16

    expert_ids = lax.broadcasted_iota(jnp.int32, (1, 1, experts), 2)
    named = routes[:, :, None] == expert_ids
    delta_ids = jnp.sum(jnp.where(named, delta_of[None, None, :], 0), axis=2)
    weight_of = jnp.sum(
        jnp.where(delta_ids[:, :, None] == expert_ids, gate_weights[:, :, None], 0.0), axis=1
    )
    weights = lax.all_gather(weight_of, "wide", axis=0, tiled=True)
    weights = lax.dynamic_slice_in_dim(weights, mine * exp_here, exp_here, axis=1)

    rows = lax.all_gather(tokens, "wide", axis=0, tiled=True)
    full = lax.all_gather(rows, "narrow", axis=1, tiled=True)
    depth = base_gate.shape[0]
    part = lax.dynamic_slice_in_dim(full, mine * depth, depth, axis=1)

    base_both = jnp.concatenate([base_gate, base_up], axis=1)
    both = lax.psum(dot32(part, base_both), "wide")
    columns = base_gate.shape[1]

    lefts = jnp.concatenate([gate_left, up_left], axis=0)
    low = lax.psum(jnp.einsum("td,edr->ter", rows, lefts, preferred_element_type=jnp.float32), "narrow")
    low = low.astype(bf16)

    mixed = 0.0
    thin = []
    for e in range(exp_here):
        gate = both[:, :columns] + dot32(low[:, e], gate_right[e])
        up = both[:, columns:] + dot32(low[:, exp_here + e], up_right[e])
        hidden = jax.nn.silu(gate) * up * weights[:, e : e + 1]
        mixed = mixed + hidden
        thin.append(dot32(hidden.astype(bf16), down_left[e]))
    mixed = lax.psum(mixed, "wide").astype(bf16)
    mixed_full = lax.all_gather(mixed, "narrow", axis=1, tiled=True)
    depth = base_down.shape[0]
    mixed_part = lax.dynamic_slice_in_dim(mixed_full, mine * depth, depth, axis=1)
    thin = lax.psum(jnp.concatenate(thin, axis=1), "narrow").astype(bf16)
    out = dot32(mixed_part, base_down) + dot32(thin, down_right.reshape(exp_here * rank, -1))
    out = lax.psum_scatter(out, "wide", scatter_dimension=0, tiled=True)
    return out.astype(bf16)


def solution(mesh):
    return jax.shard_map(
        shards,
        mesh=mesh,
        in_specs=(
            P(("groups", "wide"), "narrow"),
            P(("groups", "wide"), None),
            P(("groups", "wide"), None),
            P(),
            P("wide", "narrow"),
            P("wide", "narrow"),
            P("wide", "narrow"),
            P("wide", "narrow", None),
            P("wide", None, "narrow"),
            P("wide", "narrow", None),
            P("wide", None, "narrow"),
            P("wide", "narrow", None),
            P("wide", None, "narrow"),
        ),
        out_specs=P(("groups", "wide"), "narrow"),
        check_vma=False,
    )
```

profile of v0, /device:TPU:0, one launch (start us, length us, event | category | flops | bytes accessed | tf_op | source)
XLA Modules:
  0.0 64.2 jit_solution(18235098198761163896)
XLA Ops:
  0.0 62.6 %shard_map.127 = bf16[64,1024]{1,0:T(8,128)(2,1)} custom-call(bf16[64,1024]{1,0:T(8,128)(2,1)} %tok.1, s32[8,64]{1,0:T(8,128)} %bitcast.14, f32[8,64]{1,0:T(8,128)} %bitcast.15, s32[16]{0:T(128)} %delta.1, bf16[1024,384]{1,0:T(8,128)(2,1)} %bg_hbm.1, bf16[1024,384]{1,0:T(8,128)(2,1)} %bu_hbm.1, bf16[384,1024]{1,0:T(8,128)(2,1)} %bd_hbm.1, ...), custom_call_target="tpu_custom_call" | custom-call | tf_op jit(solution)/shard_map/pallas_call | solution.py:308
  62.6 1.6 %copy.15 = bf16[64,1024]{1,0:T(8,128)(2,1)} copy(bf16[64,1024]{1,0:T(8,128)(2,1)} %shard_map.127) | data formatting | bytes 262144
where the time goes:
time: 65 us; the launch traced here: 64.2 us
  Pallas kernels  62.6 us (96%)
  local copies, waits for them, and re-layouts  1.57 us (2%)
    pallas_call x1, Pallas kernels, fused(): pl.pallas_call(kernel, out_shape=jax.ShapeDtypeStruct((rows, out_feats),...  62.6 us
    unnamed x1, local copies, waits for them, and re-layouts  1.57 us

commit v1 on v0

v1 whole, which is shorter than its diff:
```python
import jax
import jax.numpy as jnp
from jax import lax
from jax.experimental import pallas as pl
from jax.experimental.pallas import tpu as pltpu
from jax.sharding import PartitionSpec as P


def dot32(a, b):
    return jnp.dot(a, b, preferred_element_type=jnp.float32)


def dot32t(a, b):
    return lax.dot_general(a, b, (((1,), (1,)), ((), ())), preferred_element_type=jnp.float32)


PLANE = 4

LANES = 128


ORDER = (1, 2, 0, 3)


def kernel(
    tok, routes_hbm, shares_hbm, delta, bg_hbm, bu_hbm, bd_hbm, gl_hbm, gr_hbm, ul_hbm, ur_hbm, dl_hbm, dr_hbm, out,
    routes, shares, bgu, lefts, bd, dr, gr, ur, dl,
    xcol, xw, wts, gpart, gsend, grecv, gxs, gxr, gall, apart, asend, arecv, afin,
    hst, hacc, hsend, hlo, hhi, hpl, bpart, bsend, brecv, bfin, osend, orecv, oown,
    ti_s, to_s, tok_r, wt_s, wt_r, bs_s, bs_r, g_s, g_r, x_s, x_r, f_s, f_r, a_s, a_r,
    h_s, hl_r, hh_r, hb_s, hb_r, b_s, b_r, o_s, o_r, in_s,
):
    bf16, f32 = jnp.bfloat16, jnp.float32
    count = PLANE
    w, n = lax.axis_index("wide"), lax.axis_index("narrow")
    rows = tok.shape[0]
    span, cols = gr.shape
    exp_here = delta.shape[0] // count
    rank = span // exp_here
    chunk = LANES if cols % LANES == 0 else cols
    chunks = cols // chunk
    side = w // 2
    sign = 1 - 2 * side

    def mir(j):
        return j + side * (3 - 2 * j)

    depth = mir(w)
    inner = depth == 1
    end = depth == 0
    root = n == w
    relay = n == lax.rem(w + 2, count)
    pair = n + 1 - 2 * lax.rem(n, 2)
    across = lax.rem(n + 2, count)
    inward = w + sign
    buddy = w + 1 - 2 * lax.rem(w, 2)

    def up_of(d):
        return lax.rem(w + d, count)

    pairs = [
        (tok, xcol.at[w]), (routes_hbm, routes), (shares_hbm, shares),
    ]
    for c in range(chunks):
        for k, base in enumerate((bg_hbm, bu_hbm)):
            pairs.append((base.at[:, pl.ds(c * chunk, chunk)], bgu.at[:, pl.ds((2 * c + k) * chunk, chunk)]))
    first = len(pairs)
    pairs += [(gl_hbm, lefts.at[pl.ds(0, span)]), (ul_hbm, lefts.at[pl.ds(span, span)])]
    second = len(pairs)
    pairs += [(gr_hbm, gr), (ur_hbm, ur), (dl_hbm, dl)]
    third = len(pairs)
    pairs += [(bd_hbm, bd), (dr_hbm, dr)]
    loads = [pltpu.make_async_copy(a, b, in_s.at[i]) for i, (a, b) in enumerate(pairs)]

    def copy(src, dst, ss, rs, axis, peer):
        return pltpu.make_async_remote_copy(
            src_ref=src, dst_ref=dst, send_sem=ss, recv_sem=rs,
            device_id={axis: peer}, device_id_type=pl.DeviceIdType.MESH,
        )

    barrier = pltpu.get_barrier_semaphore()
    for d in range(1, count):
        pl.semaphore_signal(barrier, inc=1, device_id={"wide": up_of(d)}, device_id_type=pl.DeviceIdType.MESH)
    for peer in (pair, across):
        pl.semaphore_signal(barrier, inc=1, device_id={"narrow": peer}, device_id_type=pl.DeviceIdType.MESH)
    for load in loads:
        load.start()
    pl.semaphore_wait(barrier, count + 1)

    own_in = copy(tok, xcol.at[w], ti_s.at[0], tok_r.at[w], "wide", inward)
    own_out = copy(tok, xcol.at[w], to_s.at[0], tok_r.at[w], "wide", buddy)

    def tok_in(b):
        return copy(xcol.at[b], xcol.at[b], ti_s.at[1], tok_r.at[b], "wide", inward)

    def tok_out(b, k):
        return copy(xcol.at[b], xcol.at[b], to_s.at[k], tok_r.at[b], "wide", buddy)

    def pair_copy(b, src):
        return copy(src, xw.at[b], bs_s.at[b, 0], bs_r.at[b], "narrow", pair)

    def across_copy(b, src):
        return copy(src, xw.at[b], bs_s.at[b, 1], bs_r.at[b], "narrow", across)

    def wt_copy(d):
        return copy(wts.at[w], wts.at[w], wt_s.at[d], wt_r.at[w], "wide", up_of(d))

    def wt_from(d):
        return copy(wts.at[up_of(d)], wts.at[up_of(d)], wt_s.at[d], wt_r.at[up_of(d)], "wide", up_of(d))

    own_in.start()

    @pl.when(jnp.logical_and(inner, jnp.logical_not(root)))
    def _():
        own_out.start()

    @pl.when(root)
    def _():
        across_copy(w, tok).start()
        pair_copy(w, tok).start()

    for load in loads[:3]:
        load.wait()
    named, ids = routes[...], jnp.zeros(routes.shape, jnp.int32)
    for e in range(delta.shape[0]):
        ids = jnp.where(named == e, delta[e], ids)
    sets = lax.broadcasted_iota(jnp.int32, wts.shape[1:], 0)
    table = jnp.zeros(sets.shape, f32)
    for k in range(routes.shape[0]):
        table = table + jnp.where(sets == ids[k : k + 1], shares[k : k + 1, :], 0.0)
    wts[w] = table

    @pl.when(root)
    def _():
        xw[w] = xcol[w]

    for load in loads[3:first]:
        load.wait()

    def part_of(c):
        return pl.ds(2 * c * chunk, 2 * chunk)

    def g_copy(b, c):
        return copy(gsend.at[b, :, part_of(c)], grecv.at[b, :, part_of(c)], g_s.at[b, c], g_r.at[b, c], "wide", buddy)

    def x_copy(b, c):
        return copy(gxs.at[b, :, part_of(c)], gxr.at[b, :, part_of(c)], x_s.at[b, c], x_r.at[b, c], "wide", inward)

    def f_copy(b, c):
        return copy(gall.at[b, :, part_of(c)], gall.at[b, :, part_of(c)], f_s.at[b, c], f_r.at[b, c], "wide", buddy)

    def arrive(j):
        b = mir(1 - depth) if j == 1 else mir(j)

        @pl.when(jnp.logical_or(root, inner))
        def _():
            tok_in(b).wait_recv()

        if j == 1:

            @pl.when(inner)
            def _():
                tok_in(b).start()

        else:

            @pl.when(jnp.logical_and(inner, jnp.logical_not(root)))
            def _():
                tok_out(b, j - 1).start()

        @pl.when(root)
        def _():
            across_copy(b, xcol.at[b]).start()
            pair_copy(b, xcol.at[b]).start()
            xw[b] = xcol[b]

    def base(j):
        b = w if j == 0 else (mir(1 - depth) if j == 1 else mir(j))

        @pl.when(jnp.logical_not(root))
        def _():
            pair_copy(b, xw.at[b]).wait_recv()

        @pl.when(relay)
        def _():
            pair_copy(b, xw.at[b]).start()

        both = dot32(xw[b], bgu[...])
        gpart[b] = both

        @pl.when(end)
        def _():
            gsend[b] = both.astype(bf16)
            for c in range(chunks):
                g_copy(b, c).start()

    def side_sum(j):
        b = mir(j)

        @pl.when(inner)
        def _():
            for c in range(chunks):
                part = slice(2 * c * chunk, 2 * (c + 1) * chunk)
                g_copy(b, c).wait_recv()
                total = gpart[b, :, part] + grecv[b, :, part].astype(f32)
                gpart[b, :, part] = total
                gxs[b, :, part] = total.astype(bf16)
                x_copy(b, c).start()

    base(0)
    arrive(1)
    arrive(2)
    base(1)
    arrive(3)
    base(2)
    base(3)

    @pl.when(jnp.logical_and(inner, root))
    def _():
        own_out.start()
        tok_out(mir(2), 1).start()
        tok_out(mir(3), 2).start()

    for d in range(1, count):
        wt_copy(d).start()
    side_sum(0)
    side_sum(1)

    @pl.when(jnp.logical_and(end, jnp.logical_not(root)))
    def _():
        for j in range(1, count):
            tok_in(mir(j)).wait_recv()

    for load in loads[first:second]:
        load.wait()

    def a_copy(k):
        return copy(asend.at[k], arecv.at[k], a_s.at[k], a_r.at[k], "narrow", (pair, across)[k])

    for b in range(count):
        apart[b] = dot32t(xcol[b], lefts[...])
    asend[0] = apart[...].astype(bf16)
    a_copy(0).start()
    side_sum(2)
    a_copy(0).wait_recv()
    apart[...] = apart[...] + arecv[0].astype(f32)
    asend[1] = apart[...].astype(bf16)
    a_copy(1).start()
    side_sum(3)
    for load in loads[second:third]:
        load.wait()
    for d in range(1, count):
        wt_from(d).wait_recv()

    def settle(b):
        @pl.when(inner)
        def _():
            for c in range(chunks):
                part = slice(2 * c * chunk, 2 * (c + 1) * chunk)
                x_copy(b, c).wait_recv()
                total = gpart[b, :, part] + gxr[b, :, part].astype(f32)
                gpart[b, :, part] = total
                gall[b, :, part] = total.astype(bf16)
                f_copy(b, c).start()

    def fetch(b):
        @pl.when(end)
        def _():
            for c in range(chunks):
                part = slice(2 * c * chunk, 2 * (c + 1) * chunk)
                f_copy(b, c).wait_recv()
                gpart[b, :, part] = gall[b, :, part].astype(f32)

    groups_of = lax.broadcasted_iota(jnp.int32, (rows, span), 1) // rank

    def spread(block):
        return jnp.concatenate(
            [jnp.where(groups_of == e, block, jnp.zeros_like(block)) for e in range(exp_here)], axis=0
        )

    def hidden_of(b):
        scales = wts[b].T
        ids = lax.broadcasted_iota(jnp.int32, scales.shape, 1)
        scale = [
            jnp.sum(jnp.where(ids == w * exp_here + e, scales, 0.0), axis=1, keepdims=True) for e in range(exp_here)
        ]
        thin_gate, thin_up = spread(afin[b, :, :span]), spread(afin[b, :, span:])
        for c in range(chunks):
            part = slice(c * chunk, (c + 1) * chunk)
            gates = gpart[b, :, 2 * c * chunk : (2 * c + 1) * chunk]
            ups = gpart[b, :, (2 * c + 1) * chunk : 2 * (c + 1) * chunk]
            more_gate, more_up = dot32(thin_gate, gr[:, part]), dot32(thin_up, ur[:, part])
            acc = None
            for e in range(exp_here):
                own = slice(e * rows, (e + 1) * rows)
                gate, up = gates + more_gate[own], ups + more_up[own]
                hidden = gate / (1.0 + jnp.exp(-gate)) * up * scale[e]
                acc = hidden if acc is None else acc + hidden
                hst[own, part] = hidden.astype(bf16)
            hacc[b, :, part] = acc
        thin = dot32t(hst[...], dl[...])
        mixed = jnp.zeros((rows, span), f32)
        for e in range(exp_here):
            mixed = mixed + jnp.where(groups_of == e, thin[e * rows : (e + 1) * rows], 0.0)
        bpart[b] = mixed

    def up_copy(b):
        return copy(hsend.at[b], hlo.at[b], h_s.at[b], hl_r.at[b], "wide", lax.rem(w + 1, count))

    def down_copy(b):
        return copy(hsend.at[b], hhi.at[b], h_s.at[b], hh_r.at[b], "wide", lax.rem(w + count - 1, count))

    def pass_on(b):
        @pl.when(w < n)
        def _():
            @pl.when(w > 0)
            def _():
                up_copy(b).wait_recv()
                hacc[b] = hacc[b] + hlo[b].astype(f32)

            hsend[b] = hacc[b].astype(bf16)
            up_copy(b).start()

        @pl.when(w > n)
        def _():
            @pl.when(w < count - 1)
            def _():
                down_copy(b).wait_recv()
                hacc[b] = hacc[b] + hhi[b].astype(f32)

            hsend[b] = hacc[b].astype(bf16)
            down_copy(b).start()

    def hpair(b):
        return copy(hpl.at[b], hpl.at[b], hb_s.at[0, b], hb_r.at[b], "narrow", pair)

    def hacross(b):
        return copy(hpl.at[b], hpl.at[b], hb_s.at[1, b], hb_r.at[b], "narrow", across)

    def collect(b):
        @pl.when(root)
        def _():
            @pl.when(w > 0)
            def _():
                up_copy(b).wait_recv()
                hacc[b] = hacc[b] + hlo[b].astype(f32)

            @pl.when(w < count - 1)
            def _():
                down_copy(b).wait_recv()
                hacc[b] = hacc[b] + hhi[b].astype(f32)

            hpl[b] = hacc[b].astype(bf16)
            hacross(b).start()
            hpair(b).start()

    settle(ORDER[0])
    settle(ORDER[1])
    a_copy(1).wait_recv()
    afin[...] = (apart[...] + arecv[1].astype(f32)).astype(bf16)
    for i in range(count):
        fetch(ORDER[i])
        hidden_of(ORDER[i])
        if i + 2 < count:
            settle(ORDER[i + 2])
        if i > 0:
            pass_on(ORDER[i - 1])

    def b_copy(k):
        return copy(bsend.at[k], brecv.at[k], b_s.at[k], b_r.at[k], "narrow", (pair, across)[k])

    bsend[0] = bpart[...].astype(bf16)
    b_copy(0).start()
    pass_on(ORDER[-1])
    for b in ORDER[:-1]:
        collect(b)
    b_copy(0).wait_recv()
    bpart[...] = bpart[...] + brecv[0].astype(f32)
    bsend[1] = bpart[...].astype(bf16)
    b_copy(1).start()
    collect(ORDER[-1])
    for load in loads[third:]:
        load.wait()
    b_copy(1).wait_recv()
    bfin[...] = (bpart[...] + brecv[1].astype(f32)).astype(bf16)

    def o_copy(b):
        return copy(osend.at[b], orecv.at[w], o_s.at[b], o_r.at[w], "wide", b)

    def o_from(s):
        return copy(osend.at[s], orecv.at[s], o_s.at[s], o_r.at[s], "wide", s)

    for b in ORDER:

        @pl.when(jnp.logical_not(root))
        def _():
            hpair(b).wait_recv()

        @pl.when(relay)
        def _():
            hpair(b).start()

        part = dot32(hpl[b], bd[...]) + dot32(bfin[b], dr[...])

        @pl.when(w == b)
        def _():
            oown[...] = part

        @pl.when(w != b)
        def _():
            osend[b] = part.astype(bf16)
            o_copy(b).start()

    total = oown[...]
    for d in range(1, count):
        s = up_of(d)
        o_from(s).wait_recv()
        total = total + orecv[s].astype(f32)
    out[...] = total.astype(bf16)

    own_in.wait_send()
    for d in range(1, count):
        wt_copy(d).wait_send()
        o_from(up_of(d)).wait_send()
    for k in range(2):
        a_copy(k).wait_send()
        b_copy(k).wait_send()

    @pl.when(inner)
    def _():
        own_out.wait_send()
        tok_in(mir(0)).wait_send()
        for j in (2, 3):
            tok_out(mir(j), j - 1).wait_send()
        for b in range(count):
            for c in range(chunks):
                x_copy(b, c).wait_send()
                f_copy(b, c).wait_send()

    @pl.when(end)
    def _():
        for b in range(count):
            for c in range(chunks):
                g_copy(b, c).wait_send()

    @pl.when(root)
    def _():
        for b in range(count):
            across_copy(b, xcol.at[b]).wait_send()
            pair_copy(b, xcol.at[b]).wait_send()
            hacross(b).wait_send()
            hpair(b).wait_send()

    @pl.when(relay)
    def _():
        for b in range(count):
            pair_copy(b, xw.at[b]).wait_send()
            hpair(b).wait_send()

    @pl.when(jnp.logical_not(root))
    def _():
        for b in range(count):
            up_copy(b).wait_send()


def fused(tokens, routes, shares, delta, bg, bu, bd, gl, gr, ul, ur, dl, dr):
    bf16, f32 = jnp.bfloat16, jnp.float32
    count = PLANE
    rows, feats = tokens.shape
    depth, cols = bg.shape
    exp_here, rank, _ = gr.shape
    span = exp_here * rank
    sets = -(-delta.shape[0] // 8) * 8
    chunks = cols // LANES if cols % LANES == 0 else 1
    sem = pltpu.SemaphoreType.DMA
    vm = pltpu.VMEM
    out_feats = bd.shape[1]
    top = routes.shape[1]
    hbm = pl.BlockSpec(memory_space=pl.ANY)
    four = sem((count,))
    grid4 = sem((count, chunks))
    return pl.pallas_call(
        kernel,
        out_shape=jax.ShapeDtypeStruct((rows, out_feats), bf16),
        in_specs=[hbm, hbm, hbm, pl.BlockSpec(memory_space=pltpu.SMEM)] + [hbm] * 9,
        out_specs=pl.BlockSpec(memory_space=pltpu.VMEM),
        scratch_shapes=[
            vm((top, rows), jnp.int32), vm((top, rows), f32),
            vm((depth, 2 * cols), bf16),
            vm((2 * span, feats), bf16),
            vm(bd.shape, bf16),
            vm((span, out_feats), bf16),
            vm((span, cols), bf16), vm((span, cols), bf16), vm((span, cols), bf16),
            vm((count, rows, feats), bf16),
            vm((count, rows, feats), bf16),
            vm((count, sets, rows), f32),
            vm((count, rows, 2 * cols), f32),
            vm((count, rows, 2 * cols), bf16),
            vm((count, rows, 2 * cols), bf16),
            vm((count, rows, 2 * cols), bf16),
            vm((count, rows, 2 * cols), bf16),
            vm((count, rows, 2 * cols), bf16),
            vm((count, rows, 2 * span), f32),
            vm((2, count, rows, 2 * span), bf16),
            vm((2, count, rows, 2 * span), bf16),
            vm((count, rows, 2 * span), bf16),
            vm((exp_here * rows, cols), bf16),
            vm((count, rows, cols), f32),
            vm((count, rows, cols), bf16),
            vm((count, rows, cols), bf16),
            vm((count, rows, cols), bf16),
            vm((count, rows, cols), bf16),
            vm((count, rows, span), f32),
            vm((2, count, rows, span), bf16),
            vm((2, count, rows, span), bf16),
            vm((count, rows, span), bf16),
            vm((count, rows, out_feats), bf16),
            vm((count, rows, out_feats), bf16),
            vm((rows, out_feats), f32),
            sem((2,)), sem((3,)), four, four, four, sem((count, 2)), four,
            grid4, grid4, grid4, grid4, grid4, grid4, sem((2,)), sem((2,)),
            four, four, four, sem((2, count)), four, sem((2,)), sem((2,)), four, four, sem((10 + 2 * chunks,)),
        ],
        compiler_params=pltpu.CompilerParams(collective_id=0, has_side_effects=True, vmem_limit_bytes=60 * 1024 * 1024),
    )(
        tokens, routes.T, shares.T, delta, bg, bu, bd,
        jnp.swapaxes(gl, 1, 2).reshape(span, feats), gr.reshape(span, cols),
        jnp.swapaxes(ul, 1, 2).reshape(span, feats), ur.reshape(span, cols),
        jnp.swapaxes(dl, 1, 2).reshape(span, cols), dr.reshape(span, out_feats),
    )


def shards(
    tokens,
    routes,
    gate_weights,
    delta_of,
    base_gate,
    base_up,
    base_down,
    gate_left,
    gate_right,
    up_left,
    up_right,
    down_left,
    down_right,
):
    if lax.axis_size("narrow") == PLANE and lax.axis_size("wide") == PLANE:
        return fused(
            tokens, routes, gate_weights, delta_of, base_gate, base_up, base_down,
            gate_left, gate_right, up_left, up_right, down_left, down_right,
        )
    exp_here, _, rank = gate_left.shape
    experts = delta_of.shape[0]
    mine = lax.axis_index("wide")
    bf16 = jnp.bfloat16

    expert_ids = lax.broadcasted_iota(jnp.int32, (1, 1, experts), 2)
    named = routes[:, :, None] == expert_ids
    delta_ids = jnp.sum(jnp.where(named, delta_of[None, None, :], 0), axis=2)
    weight_of = jnp.sum(
        jnp.where(delta_ids[:, :, None] == expert_ids, gate_weights[:, :, None], 0.0), axis=1
    )
    weights = lax.all_gather(weight_of, "wide", axis=0, tiled=True)
    weights = lax.dynamic_slice_in_dim(weights, mine * exp_here, exp_here, axis=1)

    rows = lax.all_gather(tokens, "wide", axis=0, tiled=True)
    full = lax.all_gather(rows, "narrow", axis=1, tiled=True)
    depth = base_gate.shape[0]
    part = lax.dynamic_slice_in_dim(full, mine * depth, depth, axis=1)

    base_both = jnp.concatenate([base_gate, base_up], axis=1)
    both = lax.psum(dot32(part, base_both), "wide")
    columns = base_gate.shape[1]

    lefts = jnp.concatenate([gate_left, up_left], axis=0)
    low = lax.psum(jnp.einsum("td,edr->ter", rows, lefts, preferred_element_type=jnp.float32), "narrow")
    low = low.astype(bf16)

    mixed = 0.0
    thin = []
    for e in range(exp_here):
        gate = both[:, :columns] + dot32(low[:, e], gate_right[e])
        up = both[:, columns:] + dot32(low[:, exp_here + e], up_right[e])
        hidden = jax.nn.silu(gate) * up * weights[:, e : e + 1]
        mixed = mixed + hidden
        thin.append(dot32(hidden.astype(bf16), down_left[e]))
    mixed = lax.psum(mixed, "wide").astype(bf16)
    mixed_full = lax.all_gather(mixed, "narrow", axis=1, tiled=True)
    depth = base_down.shape[0]
    mixed_part = lax.dynamic_slice_in_dim(mixed_full, mine * depth, depth, axis=1)
    thin = lax.psum(jnp.concatenate(thin, axis=1), "narrow").astype(bf16)
    out = dot32(mixed_part, base_down) + dot32(thin, down_right.reshape(exp_here * rank, -1))
    out = lax.psum_scatter(out, "wide", scatter_dimension=0, tiled=True)
    return out.astype(bf16)


def solution(mesh):
    return jax.shard_map(
        shards,
        mesh=mesh,
        in_specs=(
            P(("groups", "wide"), "narrow"),
            P(("groups", "wide"), None),
            P(("groups", "wide"), None),
            P(),
            P("wide", "narrow"),
            P("wide", "narrow"),
            P("wide", "narrow"),
            P("wide", "narrow", None),
            P("wide", None, "narrow"),
            P("wide", "narrow", None),
            P("wide", None, "narrow"),
            P("wide", "narrow", None),
            P("wide", None, "narrow"),
        ),
        out_specs=P(("groups", "wide"), "narrow"),
        check_vma=False,
    )
```

time: 65 us -> 67.3 us (1.035); the launches traced: 64.2 us -> 67.2 us
  Pallas kernels: 62.6 us -> 65.6 us
    pallas_call x1, Pallas kernels: 62.6 us -> 65.6 us  [fused(): pl.pallas_call(kernel, out_shape=jax.ShapeDtypeStruct((rows, out_feats),...]
where the time goes in v1:
time: 67.3 us; the launch traced here: 67.2 us
  Pallas kernels  65.6 us (97%)
  local copies, waits for them, and re-layouts  1.57 us (2%)
    pallas_call x1, Pallas kernels, fused(): pl.pallas_call(kernel, out_shape=jax.ShapeDtypeStruct((rows, out_feats),...  65.6 us
    unnamed x1, local copies, waits for them, and re-layouts  1.57 us

profile of v1, /device:TPU:0, one launch (start us, length us, event | category | flops | bytes accessed | tf_op | source)
XLA Modules:
  0.0 67.2 jit_solution(3762137817016537752)
XLA Ops:
  0.0 65.6 %shard_map.127 = bf16[64,1024]{1,0:T(8,128)(2,1)} custom-call(bf16[64,1024]{1,0:T(8,128)(2,1)} %tok.1, s32[8,64]{1,0:T(8,128)} %bitcast.20, f32[8,64]{1,0:T(8,128)} %bitcast.21, s32[16]{0:T(128)} %delta.1, bf16[1024,384]{1,0:T(8,128)(2,1)} %bg_hbm.1, bf16[1024,384]{1,0:T(8,128)(2,1)} %bu_hbm.1, bf16[384,1024]{1,0:T(8,128)(2,1)} %bd_hbm.1, ...), custom_call_target="tpu_custom_call" | custom-call | tf_op jit(solution)/shard_map/pallas_call | solution.py:482
  65.6 1.6 %copy.15 = bf16[64,1024]{1,0:T(8,128)(2,1)} copy(bf16[64,1024]{1,0:T(8,128)(2,1)} %shard_map.127) | data formatting | bytes 262144

commit v2 on v1

--- a/solution.py
+++ b/solution.py
@@ -25,10 +25,10 @@
 def kernel(
     tok, routes_hbm, shares_hbm, delta, bg_hbm, bu_hbm, bd_hbm, gl_hbm, gr_hbm, ul_hbm, ur_hbm, dl_hbm, dr_hbm, out,
     routes, shares, bgu, lefts, bd, dr, gr, ur, dl,
-    xcol, xw, wts, gpart, gsend, grecv, gxs, gxr, gall, apart, asend, arecv, afin,
-    hst, hacc, hsend, hlo, hhi, hpl, bpart, bsend, brecv, bfin, osend, orecv, oown,
+    xcol, xw, wts, gpart, gsend, grecv, gxs, gxr, gall, apart, asend, arecv,
+    hst, hacc, hsend, hrecv, hpl, bpart, bsend, brecv, osend, orecv, oown,
     ti_s, to_s, tok_r, wt_s, wt_r, bs_s, bs_r, g_s, g_r, x_s, x_r, f_s, f_r, a_s, a_r,
-    h_s, hl_r, hh_r, hb_s, hb_r, b_s, b_r, o_s, o_r, in_s,
+    h_s, h_r, hb_s, hb_r, b_s, b_r, o_s, o_r, in_s,
 ):
     bf16, f32 = jnp.bfloat16, jnp.float32
     count = PLANE
@@ -52,6 +52,7 @@
     relay = n == lax.rem(w + 2, count)
     pair = n + 1 - 2 * lax.rem(n, 2)
     across = lax.rem(n + 2, count)
+    beside = (pair, across, lax.rem(pair + 2, count))
     inward = w + sign
     buddy = w + 1 - 2 * lax.rem(w, 2)
 
@@ -61,11 +62,11 @@
     pairs = [
         (tok, xcol.at[w]), (routes_hbm, routes), (shares_hbm, shares),
     ]
+    pairs += [(gl_hbm, lefts.at[pl.ds(0, span)]), (ul_hbm, lefts.at[pl.ds(span, span)])]
+    first = len(pairs)
     for c in range(chunks):
         for k, base in enumerate((bg_hbm, bu_hbm)):
             pairs.append((base.at[:, pl.ds(c * chunk, chunk)], bgu.at[:, pl.ds((2 * c + k) * chunk, chunk)]))
-    first = len(pairs)
-    pairs += [(gl_hbm, lefts.at[pl.ds(0, span)]), (ul_hbm, lefts.at[pl.ds(span, span)])]
     second = len(pairs)
     pairs += [(gr_hbm, gr), (ur_hbm, ur), (dl_hbm, dl)]
     third = len(pairs)
@@ -81,17 +82,19 @@
     barrier = pltpu.get_barrier_semaphore()
     for d in range(1, count):
         pl.semaphore_signal(barrier, inc=1, device_id={"wide": up_of(d)}, device_id_type=pl.DeviceIdType.MESH)
-    for peer in (pair, across):
+    for peer in beside:
         pl.semaphore_signal(barrier, inc=1, device_id={"narrow": peer}, device_id_type=pl.DeviceIdType.MESH)
     for load in loads:
         load.start()
-    pl.semaphore_wait(barrier, count + 1)
+    pl.semaphore_wait(barrier, 2 * (count - 1))
 
     own_in = copy(tok, xcol.at[w], ti_s.at[0], tok_r.at[w], "wide", inward)
     own_out = copy(tok, xcol.at[w], to_s.at[0], tok_r.at[w], "wide", buddy)
 
+    own_far = copy(tok, xcol.at[w], ti_s.at[1], tok_r.at[w], "wide", count - 1 - buddy)
+
     def tok_in(b):
-        return copy(xcol.at[b], xcol.at[b], ti_s.at[1], tok_r.at[b], "wide", inward)
+        return copy(xcol.at[b], xcol.at[b], ti_s.at[1], tok_r.at[b], "wide", buddy)
 
     def tok_out(b, k):
         return copy(xcol.at[b], xcol.at[b], to_s.at[k], tok_r.at[b], "wide", buddy)
@@ -109,6 +112,10 @@
         return copy(wts.at[up_of(d)], wts.at[up_of(d)], wt_s.at[d], wt_r.at[up_of(d)], "wide", up_of(d))
 
     own_in.start()
+
+    @pl.when(end)
+    def _():
+        own_far.start()
 
     @pl.when(jnp.logical_and(inner, jnp.logical_not(root)))
     def _():
@@ -134,8 +141,28 @@
     def _():
         xw[w] = xcol[w]
 
+    def a_copy(k, b):
+        return copy(asend.at[b], arecv.at[k, b], a_s.at[k, b], a_r.at[k, b], "narrow", beside[k])
+
+    def low(j):
+        b = w if j == 0 else (mir(1 - depth) if j == 1 else mir(j))
+        if j > 0:
+
+            @pl.when(jnp.logical_and(end, jnp.logical_not(root)))
+            def _():
+                tok_in(b).wait_recv()
+
+        thin = dot32t(xcol[b], lefts[...])
+        apart[b] = thin
+        asend[b] = thin.astype(bf16)
+        for k in range(3):
+            a_copy(k, b).start()
+
     for load in loads[3:first]:
         load.wait()
+    low(0)
+    for load in loads[first:second]:
+        load.wait()
 
     def part_of(c):
         return pl.ds(2 * c * chunk, 2 * chunk)
@@ -149,26 +176,28 @@
     def f_copy(b, c):
         return copy(gall.at[b, :, part_of(c)], gall.at[b, :, part_of(c)], f_s.at[b, c], f_r.at[b, c], "wide", buddy)
 
-    def arrive(j):
+    def arrive(j, who):
         b = mir(1 - depth) if j == 1 else mir(j)
 
-        @pl.when(jnp.logical_or(root, inner))
+        @pl.when(jnp.logical_and(who, jnp.logical_or(root, inner)))
         def _():
             tok_in(b).wait_recv()
 
-        if j == 1:
-
-            @pl.when(inner)
-            def _():
-                tok_in(b).start()
-
-        else:
+        if j > 1 and who is inner:
 
             @pl.when(jnp.logical_and(inner, jnp.logical_not(root)))
             def _():
                 tok_out(b, j - 1).start()
 
-        @pl.when(root)
+            @pl.when(jnp.logical_and(inner, root))
+            def _():
+                if j == 2:
+                    own_out.start()
+                else:
+                    tok_out(mir(2), 1).start()
+                    tok_out(b, 2).start()
+
+        @pl.when(jnp.logical_and(who, root))
         def _():
             across_copy(b, xcol.at[b]).start()
             pair_copy(b, xcol.at[b]).start()
@@ -208,46 +237,21 @@
                 x_copy(b, c).start()
 
     base(0)
-    arrive(1)
-    arrive(2)
-    base(1)
-    arrive(3)
-    base(2)
-    base(3)
-
-    @pl.when(jnp.logical_and(inner, root))
-    def _():
-        own_out.start()
-        tok_out(mir(2), 1).start()
-        tok_out(mir(3), 2).start()
-
+    for j in (1, 2, 3):
+        arrive(j, inner)
+    for j in (1, 2, 3):
+        arrive(j, end)
+        base(j)
     for d in range(1, count):
         wt_copy(d).start()
     side_sum(0)
     side_sum(1)
-
-    @pl.when(jnp.logical_and(end, jnp.logical_not(root)))
-    def _():
-        for j in range(1, count):
-            tok_in(mir(j)).wait_recv()
-
-    for load in loads[first:second]:
-        load.wait()
-
-    def a_copy(k):
-        return copy(asend.at[k], arecv.at[k], a_s.at[k], a_r.at[k], "narrow", (pair, across)[k])
-
-    for b in range(count):
-        apart[b] = dot32t(xcol[b], lefts[...])
-    asend[0] = apart[...].astype(bf16)
-    a_copy(0).start()
+    low(1)
+    low(2)
+    low(3)
     side_sum(2)
-    a_copy(0).wait_recv()
-    apart[...] = apart[...] + arecv[0].astype(f32)
-    asend[1] = apart[...].astype(bf16)
-    a_copy(1).start()
     side_sum(3)
-    for load in loads[second:third]:
+    for load in loads[second:]:
         load.wait()
     for d in range(1, count):
         wt_from(d).wait_recv()
@@ -278,13 +282,21 @@
             [jnp.where(groups_of == e, block, jnp.zeros_like(block)) for e in range(exp_here)], axis=0
         )
 
+    def b_copy(k, b):
+        return copy(bsend.at[b], brecv.at[k, b], b_s.at[k, b], b_r.at[k, b], "narrow", beside[k])
+
     def hidden_of(b):
         scales = wts[b].T
         ids = lax.broadcasted_iota(jnp.int32, scales.shape, 1)
         scale = [
             jnp.sum(jnp.where(ids == w * exp_here + e, scales, 0.0), axis=1, keepdims=True) for e in range(exp_here)
         ]
-        thin_gate, thin_up = spread(afin[b, :, :span]), spread(afin[b, :, span:])
+        low_sum = apart[b]
+        for k in range(3):
+            a_copy(k, b).wait_recv()
+            low_sum = low_sum + arecv[k, b].astype(f32)
+        low_sum = low_sum.astype(bf16)
+        thin_gate, thin_up = spread(low_sum[:, :span]), spread(low_sum[:, span:])
         for c in range(chunks):
             part = slice(c * chunk, (c + 1) * chunk)
             gates = gpart[b, :, 2 * c * chunk : (2 * c + 1) * chunk]
@@ -303,33 +315,21 @@
         for e in range(exp_here):
             mixed = mixed + jnp.where(groups_of == e, thin[e * rows : (e + 1) * rows], 0.0)
         bpart[b] = mixed
-
-    def up_copy(b):
-        return copy(hsend.at[b], hlo.at[b], h_s.at[b], hl_r.at[b], "wide", lax.rem(w + 1, count))
-
-    def down_copy(b):
-        return copy(hsend.at[b], hhi.at[b], h_s.at[b], hh_r.at[b], "wide", lax.rem(w + count - 1, count))
+        bsend[b] = mixed.astype(bf16)
+        for k in range(3):
+            b_copy(k, b).start()
+
+    def h_copy(b):
+        return copy(hsend.at[b], hrecv.at[w, b], h_s.at[b], h_r.at[w, b], "wide", n)
+
+    def h_from(k, b):
+        return copy(hsend.at[b], hrecv.at[k, b], h_s.at[b], h_r.at[k, b], "wide", k)
 
     def pass_on(b):
-        @pl.when(w < n)
-        def _():
-            @pl.when(w > 0)
-            def _():
-                up_copy(b).wait_recv()
-                hacc[b] = hacc[b] + hlo[b].astype(f32)
-
+        @pl.when(jnp.logical_not(root))
+        def _():
             hsend[b] = hacc[b].astype(bf16)
-            up_copy(b).start()
-
-        @pl.when(w > n)
-        def _():
-            @pl.when(w < count - 1)
-            def _():
-                down_copy(b).wait_recv()
-                hacc[b] = hacc[b] + hhi[b].astype(f32)
-
-            hsend[b] = hacc[b].astype(bf16)
-            down_copy(b).start()
+            h_copy(b).start()
 
     def hpair(b):
         return copy(hpl.at[b], hpl.at[b], hb_s.at[0, b], hb_r.at[b], "narrow", pair)
@@ -340,96 +340,74 @@
     def collect(b):
         @pl.when(root)
         def _():
-            @pl.when(w > 0)
-            def _():
-                up_copy(b).wait_recv()
-                hacc[b] = hacc[b] + hlo[b].astype(f32)
-
-            @pl.when(w < count - 1)
-            def _():
-                down_copy(b).wait_recv()
-                hacc[b] = hacc[b] + hhi[b].astype(f32)
-
-            hpl[b] = hacc[b].astype(bf16)
+            whole = hacc[b]
+            for d in range(1, count):
+                h_from(up_of(d), b).wait_recv()
+                whole = whole + hrecv[up_of(d), b].astype(f32)
+            hpl[b] = whole.astype(bf16)
             hacross(b).start()
             hpair(b).start()
 
+    def o_copy(b):
+        return copy(osend.at[b], orecv.at[w], o_s.at[b], o_r.at[w], "wide", b)
+
+    def o_from(k):
+        return copy(osend.at[k], orecv.at[k], o_s.at[k], o_r.at[k], "wide", k)
+
+    def project(b):
+        @pl.when(jnp.logical_not(root))
+        def _():
+            hpair(b).wait_recv()
+
+        @pl.when(relay)
+        def _():
+            hpair(b).start()
+
+        thin = bpart[b]
+        for k in range(3):
+            b_copy(k, b).wait_recv()
+            thin = thin + brecv[k, b].astype(f32)
+        part = dot32(hpl[b], bd[...]) + dot32(thin.astype(bf16), dr[...])
+
+        @pl.when(w == b)
+        def _():
+            oown[...] = part
+
+        @pl.when(w != b)
+        def _():
+            osend[b] = part.astype(bf16)
+            o_copy(b).start()
+
     settle(ORDER[0])
     settle(ORDER[1])
-    a_copy(1).wait_recv()
-    afin[...] = (apart[...] + arecv[1].astype(f32)).astype(bf16)
     for i in range(count):
         fetch(ORDER[i])
         hidden_of(ORDER[i])
+        pass_on(ORDER[i])
         if i + 2 < count:
             settle(ORDER[i + 2])
-        if i > 0:
-            pass_on(ORDER[i - 1])
-
-    def b_copy(k):
-        return copy(bsend.at[k], brecv.at[k], b_s.at[k], b_r.at[k], "narrow", (pair, across)[k])
-
-    bsend[0] = bpart[...].astype(bf16)
-    b_copy(0).start()
-    pass_on(ORDER[-1])
-    for b in ORDER[:-1]:
+    for b in ORDER:
         collect(b)
-    b_copy(0).wait_recv()
-    bpart[...] = bpart[...] + brecv[0].astype(f32)
-    bsend[1] = bpart[...].astype(bf16)
-    b_copy(1).start()
-    collect(ORDER[-1])
-    for load in loads[third:]:
-        load.wait()
-    b_copy(1).wait_recv()
-    bfin[...] = (bpart[...] + brecv[1].astype(f32)).astype(bf16)
-
-    def o_copy(b):
-        return copy(osend.at[b], orecv.at[w], o_s.at[b], o_r.at[w], "wide", b)
-
-    def o_from(s):
-        return copy(osend.at[s], orecv.at[s], o_s.at[s], o_r.at[s], "wide", s)
-
-    for b in ORDER:
-
-        @pl.when(jnp.logical_not(root))
-        def _():
-            hpair(b).wait_recv()
-
-        @pl.when(relay)
-        def _():
-            hpair(b).start()
-
-        part = dot32(hpl[b], bd[...]) + dot32(bfin[b], dr[...])
-
-        @pl.when(w == b)
-        def _():
-            oown[...] = part
-
-        @pl.when(w != b)
-        def _():
-            osend[b] = part.astype(bf16)
-            o_copy(b).start()
-
+        project(b)
     total = oown[...]
     for d in range(1, count):
-        s = up_of(d)
-        o_from(s).wait_recv()
-        total = total + orecv[s].astype(f32)
+        k = up_of(d)
+        o_from(k).wait_recv()
+        total = total + orecv[k].astype(f32)
     out[...] = total.astype(bf16)
 
     own_in.wait_send()
     for d in range(1, count):
         wt_copy(d).wait_send()
         o_from(up_of(d)).wait_send()
-    for k in range(2):
-        a_copy(k).wait_send()
-        b_copy(k).wait_send()
+    for k in range(3):
+        for b in range(count):
+            a_copy(k, b).wait_send()
+            b_copy(k, b).wait_send()
 
     @pl.when(inner)
     def _():
         own_out.wait_send()
-        tok_in(mir(0)).wait_send()
         for j in (2, 3):
             tok_out(mir(j), j - 1).wait_send()
         for b in range(count):
@@ -439,6 +417,7 @@
 
     @pl.when(end)
     def _():
+        own_far.wait_send()
         for b in range(count):
             for c in range(chunks):
                 g_copy(b, c).wait_send()
@@ -460,7 +439,7 @@
     @pl.when(jnp.logical_not(root))
     def _():
         for b in range(count):
-            up_copy(b).wait_send()
+            h_copy(b).wait_send()
 
 
 def fused(tokens, routes, shares, delta, bg, bu, bd, gl, gr, ul, ur, dl, dr):
@@ -477,7 +456,7 @@
     out_feats = bd.shape[1]
     top = routes.shape[1]
     hbm = pl.BlockSpec(memory_space=pl.ANY)
-    four = sem((count,))
+    four, three = sem((count,)), sem((3, count))
     grid4 = sem((count, chunks))
     return pl.pallas_call(
         kernel,
@@ -501,25 +480,22 @@
             vm((count, rows, 2 * cols), bf16),
             vm((count, rows, 2 * cols), bf16),
             vm((count, rows, 2 * span), f32),
-            vm((2, count, rows, 2 * span), bf16),
-            vm((2, count, rows, 2 * span), bf16),
             vm((count, rows, 2 * span), bf16),
+            vm((3, count, rows, 2 * span), bf16),
             vm((exp_here * rows, cols), bf16),
             vm((count, rows, cols), f32),
             vm((count, rows, cols), bf16),
-            vm((count, rows, cols), bf16),
-            vm((count, rows, cols), bf16),
+            vm((count, count, rows, cols), bf16),
             vm((count, rows, cols), bf16),
             vm((count, rows, span), f32),
-            vm((2, count, rows, span), bf16),
-            vm((2, count, rows, span), bf16),
             vm((count, rows, span), bf16),
+            vm((3, count, rows, span), bf16),
             vm((count, rows, out_feats), bf16),
             vm((count, rows, out_feats), bf16),
             vm((rows, out_feats), f32),
             sem((2,)), sem((3,)), four, four, four, sem((count, 2)), four,
-            grid4, grid4, grid4, grid4, grid4, grid4, sem((2,)), sem((2,)),
-            four, four, four, sem((2, count)), four, sem((2,)), sem((2,)), four, four, sem((10 + 2 * chunks,)),
+            grid4, grid4, grid4, grid4, grid4, grid4, three, three,
+            four, sem((count, count)), sem((2, count)), four, three, three, four, four, sem((10 + 2 * chunks,)),
         ],
         compiler_params=pltpu.CompilerParams(collective_id=0, has_side_effects=True, vmem_limit_bytes=60 * 1024 * 1024),
     )(

time: 67.3 us -> 64.1 us (0.952)
  Pallas kernels: 65.6 us -> 62.4 us
    pallas_call x1, Pallas kernels: 65.6 us -> 62.4 us  [fused(): pl.pallas_call(kernel, out_shape=jax.ShapeDtypeStruct((rows, out_feats),...]
where the time goes in v2:
time: 64.1 us; the launch traced here: 64 us
  Pallas kernels  62.4 us (97%)
  local copies, waits for them, and re-layouts  1.57 us (2%)
    pallas_call x1, Pallas kernels, fused(): pl.pallas_call(kernel, out_shape=jax.ShapeDtypeStruct((rows, out_feats),...  62.4 us
    unnamed x1, local copies, waits for them, and re-layouts  1.57 us

profile of v2, /device:TPU:0, one launch (start us, length us, event | category | flops | bytes accessed | tf_op | source)
XLA Modules:
  0.0 64.0 jit_solution(3738336173678756)
XLA Ops:
  0.0 62.4 %shard_map.127 = bf16[64,1024]{1,0:T(8,128)(2,1)} custom-call(bf16[64,1024]{1,0:T(8,128)(2,1)} %tok.1, s32[8,64]{1,0:T(8,128)} %bitcast.20, f32[8,64]{1,0:T(8,128)} %bitcast.21, s32[16]{0:T(128)} %delta.1, bf16[1024,384]{1,0:T(8,128)(2,1)} %bg_hbm.1, bf16[1024,384]{1,0:T(8,128)(2,1)} %bu_hbm.1, bf16[384,1024]{1,0:T(8,128)(2,1)} %bd_hbm.1, ...), custom_call_target="tpu_custom_call" | custom-call | tf_op jit(solution)/shard_map/pallas_call | solution.py:461
  62.4 1.6 %copy.15 = bf16[64,1024]{1,0:T(8,128)(2,1)} copy(bf16[64,1024]{1,0:T(8,128)(2,1)} %shard_map.127) | data formatting | bytes 262144

commit v3 on v2

--- a/solution.py
+++ b/solution.py
@@ -117,7 +117,7 @@
     def _():
         own_far.start()
 
-    @pl.when(jnp.logical_and(inner, jnp.logical_not(root)))
+    @pl.when(inner)
     def _():
         own_out.start()
 
@@ -185,17 +185,9 @@
 
         if j > 1 and who is inner:
 
-            @pl.when(jnp.logical_and(inner, jnp.logical_not(root)))
+            @pl.when(inner)
             def _():
                 tok_out(b, j - 1).start()
-
-            @pl.when(jnp.logical_and(inner, root))
-            def _():
-                if j == 2:
-                    own_out.start()
-                else:
-                    tok_out(mir(2), 1).start()
-                    tok_out(b, 2).start()
 
         @pl.when(jnp.logical_and(who, root))
         def _():
@@ -378,14 +370,12 @@
             osend[b] = part.astype(bf16)
             o_copy(b).start()
 
-    settle(ORDER[0])
-    settle(ORDER[1])
+    for b in ORDER:
+        settle(b)
     for i in range(count):
         fetch(ORDER[i])
         hidden_of(ORDER[i])
         pass_on(ORDER[i])
-        if i + 2 < count:
-            settle(ORDER[i + 2])
     for b in ORDER:
         collect(b)
         project(b)

time: 64.1 us -> 62 us (0.967)
  Pallas kernels: 62.4 us -> 60.2 us
    pallas_call x1, Pallas kernels: 62.4 us -> 60.2 us  [fused(): pl.pallas_call(kernel, out_shape=jax.ShapeDtypeStruct((rows, out_feats),...]
where the time goes in v3:
time: 62 us; the launch traced here: 61.8 us
  Pallas kernels  60.2 us (97%)
  local copies, waits for them, and re-layouts  1.57 us (3%)
    pallas_call x1, Pallas kernels, fused(): pl.pallas_call(kernel, out_shape=jax.ShapeDtypeStruct((rows, out_feats),...  60.2 us
    unnamed x1, local copies, waits for them, and re-layouts  1.57 us

profile of v3, /device:TPU:0, one launch (start us, length us, event | category | flops | bytes accessed | tf_op | source)
XLA Modules:
  0.0 61.8 jit_solution(3871342701298397752)
XLA Ops:
  0.0 60.2 %shard_map.127 = bf16[64,1024]{1,0:T(8,128)(2,1)} custom-call(bf16[64,1024]{1,0:T(8,128)(2,1)} %tok.1, s32[8,64]{1,0:T(8,128)} %bitcast.20, f32[8,64]{1,0:T(8,128)} %bitcast.21, s32[16]{0:T(128)} %delta.1, bf16[1024,384]{1,0:T(8,128)(2,1)} %bg_hbm.1, bf16[1024,384]{1,0:T(8,128)(2,1)} %bu_hbm.1, bf16[384,1024]{1,0:T(8,128)(2,1)} %bd_hbm.1, ...), custom_call_target="tpu_custom_call" | custom-call | tf_op jit(solution)/shard_map/pallas_call | solution.py:451
  60.2 1.6 %copy.15 = bf16[64,1024]{1,0:T(8,128)(2,1)} copy(bf16[64,1024]{1,0:T(8,128)(2,1)} %shard_map.127) | data formatting | bytes 262144

commit v4 on v3

--- a/solution.py
+++ b/solution.py
@@ -136,6 +136,8 @@
     for k in range(routes.shape[0]):
         table = table + jnp.where(sets == ids[k : k + 1], shares[k : k + 1, :], 0.0)
     wts[w] = table
+    for d in range(1, count):
+        wt_copy(d).start()
 
     @pl.when(root)
     def _():
@@ -234,8 +236,6 @@
     for j in (1, 2, 3):
         arrive(j, end)
         base(j)
-    for d in range(1, count):
-        wt_copy(d).start()
     side_sum(0)
     side_sum(1)
     low(1)

time: 62 us -> 58.9 us (0.950)
  the two profiles are of different devices: /device:TPU:0 before, /device:TPU:26 now
where the time goes in v4:
time: 58.9 us; the launch traced here: 58.7 us
  Pallas kernels  57.2 us (97%)
  local copies, waits for them, and re-layouts  1.57 us (3%)
    pallas_call x1, Pallas kernels, fused(): pl.pallas_call(kernel, out_shape=jax.ShapeDtypeStruct((rows, out_feats),...  57.2 us
    unnamed x1, local copies, waits for them, and re-layouts  1.57 us

profile of v4, /device:TPU:26, one launch (start us, length us, event | category | flops | bytes accessed | tf_op | source)
XLA Modules:
  0.0 58.7 jit_solution(18176179646550606378)
XLA Ops:
  0.0 57.2 %shard_map.127 = bf16[64,1024]{1,0:T(8,128)(2,1)} custom-call(bf16[64,1024]{1,0:T(8,128)(2,1)} %tok.1, s32[8,64]{1,0:T(8,128)} %bitcast.20, f32[8,64]{1,0:T(8,128)} %bitcast.21, s32[16]{0:T(128)} %delta.1, bf16[1024,384]{1,0:T(8,128)(2,1)} %bg_hbm.1, bf16[1024,384]{1,0:T(8,128)(2,1)} %bu_hbm.1, bf16[384,1024]{1,0:T(8,128)(2,1)} %bd_hbm.1, ...), custom_call_target="tpu_custom_call" | custom-call | tf_op jit(solution)/shard_map/pallas_call | solution.py:451
  57.2 1.6 %copy.15 = bf16[64,1024]{1,0:T(8,128)(2,1)} copy(bf16[64,1024]{1,0:T(8,128)(2,1)} %shard_map.127) | data formatting | bytes 262144
